TPU v7x, 256 devices: a whole 4x4x8 slice. The times are simulated.
256 devices in a mesh: grp: 4 (over z_lo, core), ctx: 16 (over z_hi, y), wid: 4 (over x).
Axes of the slice: x: 4, y: 4, z: 8 (z_hi: 4, z_lo: 2; z = z_hi * 2 + z_lo), core: 2. Of those that a mesh axis runs over, the one named last changes fastest.
Arguments:
- query: bfloat16 [256, 64, 128], P(None, 'wid'), may hold values from -64 to 64
- keys: bfloat16 [4, 4096, 8, 128], P(None, ('grp', 'ctx'), 'wid'), may hold values from -64 to 64
- values: bfloat16 [4, 4096, 8, 128], P(None, ('grp', 'ctx'), 'wid'), may hold values from -6 to 6
- lengths: int32 [4, 64], replicated, may hold values from 32 to 64
- query_pos: int32 [256], replicated, may hold values from 1024 to 4095
- resid: bfloat16 [256, 5120], P('wid', ('grp', 'ctx')), may hold values from -1.1953125 to 1.1953125
- out_weight: bfloat16 [8192, 5120], P('wid', ('grp', 'ctx')), may hold values from -0.0625 to 0.0625
- enc_weight: bfloat16 [5120, 24576], P('wid', ('grp', 'ctx')), may hold values from -0.078125 to 0.078125
- enc_bias: float32 [24576], P(('grp', 'ctx')), may hold values from -3 to 3
- dec_weight: bfloat16 [24576, 5120], P(('grp', 'ctx'), 'wid'), may hold values from -0.078125 to 0.078125
- dec_bias: float32 [5120], P('wid'), may hold values from -3 to 3
Outputs:
- layer_out: bfloat16 [256, 5120], P('wid', ('grp', 'ctx'))
- enc_grad: bfloat16 [5120, 24576], P('wid', ('grp', 'ctx'))
- enc_bias_grad: float32 [24576], P(('grp', 'ctx'))
- dec_grad: bfloat16 [24576, 5120], P(('grp', 'ctx'), 'wid')
- dec_bias_grad: float32 [5120], P('wid')
Inputs may be any that keep to these rules, and one draw needn't show every extreme that they name: `lengths`: live slots of a shard are its first ones.
All inputs are finite; a program needn't handle non-finite values.
Results may differ from a plain program's by a relative error of at most 0.024.
Values may be sent and summed in bfloat16 or wider, within the bound.
No kernel may reach another device: no remote copies, remote signals or barrier semaphores. Data moves between devices by JAX's collectives and lax.ppermute only.
A program may use at most 128 MiB of HBM per device.

v0:
```python
import jax
import jax.numpy as jnp
from jax import lax
from jax.sharding import Mesh
from jax.sharding import PartitionSpec as P

HD = 128
GRP_CTX = ("grp_0", "grp_1", "ctx_0", "ctx_1")


def combined_by_axis(shard, axes, combine):
    for axis in axes:
        pieces = jax.tree.map(
            lambda part, kind: lax.all_gather(part.astype(kind), axis),
            shard,
            (jnp.bfloat16, jnp.bfloat16, jnp.bfloat16),
        )
        widened = [
            jax.tree.map(lambda part, own: part[k].astype(own.dtype), pieces, shard)
            for k in range(lax.axis_size(axis))
        ]
        shard = widened[0]
        for theirs in widened[1:]:
            shard = combine(shard, theirs)
    return shard


def in_blocks(shard, dim, length):
    before, after = (shard.shape[:dim], shard.shape[dim + 1 :])
    return jnp.moveaxis(shard.reshape(*before, length, -1, *after), dim, 0)


def summed_on_arrival(shard, axis, dim):
    length = lax.axis_size(axis)
    blocks = lax.all_to_all(in_blocks(shard, dim, length), axis, 0, 0, tiled=True)
    return jnp.sum(blocks.astype(jnp.float32), axis=0)


def from_everyone(shard, axis):
    copies = jnp.broadcast_to(shard, (lax.axis_size(axis), *shard.shape))
    return lax.all_to_all(copies, axis, split_axis=0, concat_axis=0, tiled=True)


def taken_together(shard, axis):
    everything = from_everyone(shard, axis)
    return jnp.sum(everything.astype(jnp.float32), axis=0)


def sent_and_summed(shard, axis, dim):
    length = lax.axis_size(axis)
    blocks = lax.all_to_all(in_blocks(shard, dim, length), axis, 0, 0, tiled=True)
    return jnp.sum(blocks, axis=0)


def combine(earlier, later):
    peak_a, sum_a, weighted_a = earlier
    peak_b, sum_b, weighted_b = later
    peak = jnp.maximum(peak_a, peak_b)
    factor_a = jnp.exp(peak_a - peak)
    factor_b = jnp.exp(peak_b - peak)
    weight_sum = sum_a * factor_a + sum_b * factor_b
    weighted = weighted_a * factor_a[..., None] + weighted_b * factor_b[..., None]
    return (peak, weight_sum, weighted)


def body(
    query,
    keys,
    values,
    lengths,
    query_pos,
    resid,
    out_weight,
    enc_weight,
    enc_bias,
    dec_weight,
    dec_bias,
):
    seq_count, slot_count, kv_local, head_dim = keys.shape
    row_count = query.shape[0]
    heads_local = query.shape[1]
    group_size = heads_local // kv_local
    rows_each = row_count // seq_count
    shard_pos = lax.axis_index(GRP_CTX)
    shard_ids = jnp.arange(lengths.shape[1], dtype=jnp.int32)
    offset = jnp.sum(jnp.where(shard_ids[None, :] < shard_pos, lengths, 0), axis=1)
    live_count = jnp.sum(jnp.where(shard_ids[None, :] == shard_pos, lengths, 0), axis=1)
    slot_ids = jnp.arange(slot_count, dtype=jnp.int32)
    key_pos = offset[:, None] + slot_ids[None, :]
    live_slot = slot_ids[None, :] < live_count[:, None]
    row_position = query_pos.reshape(seq_count, rows_each)
    visible = live_slot[:, None, :] & (key_pos[:, None, :] <= row_position[:, :, None])
    visible_mask = visible[:, :, None, None, :]
    q_view = query.reshape(seq_count, rows_each, kv_local, group_size, head_dim)
    scores = jnp.einsum(
        "srkgd,sjkd->srkgj", q_view, keys, preferred_element_type=jnp.float32
    ) * HD ** (-0.5)
    local_peak = jnp.max(jnp.where(visible_mask, scores, -1e30), axis=-1)
    weights = jnp.where(visible_mask, jnp.exp(scores - local_peak[..., None]), 0.0)
    weight_sum = jnp.sum(weights, axis=-1)
    weights_low = weights.astype(jnp.bfloat16)
    weighted = jnp.einsum(
        "srkgj,sjkd->srkgd", weights_low, values, preferred_element_type=jnp.float32
    )
    weight_sum, weighted = (weight_sum, weighted)
    peak, weight_sum, weighted = combined_by_axis(
        (local_peak, weight_sum, weighted), GRP_CTX, combine
    )
    attention = (weighted / weight_sum[..., None]).astype(jnp.bfloat16)
    attention = attention.reshape(row_count, heads_local * head_dim)
    projected = jnp.dot(attention, out_weight, preferred_element_type=jnp.float32)
    mixed = summed_on_arrival(projected.astype(jnp.bfloat16), "wid", 0)
    layer_out = (mixed + resid.astype(jnp.float32)).astype(jnp.bfloat16)
    wide_rows = lax.all_gather(layer_out, GRP_CTX, axis=1, tiled=True)
    block = lax.all_to_all(wide_rows, "wid", split_axis=1, concat_axis=0, tiled=True)
    enc_part = jnp.dot(block, enc_weight, preferred_element_type=jnp.float32)
    preact = taken_together(enc_part.astype(jnp.bfloat16), "wid").astype(jnp.float32) + enc_bias
    latents = (jax.nn.softplus(4.0 * preact) * 0.25).astype(jnp.bfloat16)
    row_scale = row_count ** (-0.5)
    recon = sent_and_summed(
        jnp.dot(latents, dec_weight, preferred_element_type=jnp.float32), GRP_CTX, 0
    )
    piece_len = recon.shape[0]
    target = lax.dynamic_slice_in_dim(block, shard_pos * piece_len, piece_len, 0).astype(
        jnp.float32
    )
    scaled_error = ((recon + dec_bias - target) * row_scale).astype(jnp.bfloat16)
    error_all = lax.all_gather(scaled_error, GRP_CTX, axis=0, tiled=True)
    dec_bias_grad = jnp.sum(error_all, axis=0, dtype=jnp.float32)
    latent_part = lax.dot_general(
        error_all, dec_weight, (((1,), (1,)), ((), ())), preferred_element_type=jnp.float32
    )
    dec_grad = lax.dot_general(
        latents, error_all, (((0,), (0,)), ((), ())), preferred_element_type=jnp.float32
    )
    latent_grad = taken_together(latent_part.astype(jnp.bfloat16), "wid").astype(jnp.float32)
    preact_grad = (latent_grad * jax.nn.sigmoid(4.0 * preact)).astype(jnp.bfloat16)
    enc_grad = lax.dot_general(
        block, preact_grad, (((0,), (0,)), ((), ())), preferred_element_type=jnp.float32
    ).astype(jnp.bfloat16)
    enc_bias_grad = jnp.sum(preact_grad, axis=0, dtype=jnp.float32)
    return (layer_out, enc_grad, enc_bias_grad, dec_grad.astype(jnp.bfloat16), dec_bias_grad)


def solution(mesh):
    torus = Mesh(
        mesh.devices.reshape(2, 2, 4, 4, mesh.shape["wid"]),
        ("grp_0", "grp_1", "ctx_0", "ctx_1", "wid"),
    )
    in_specs = (
        P(None, "wid", None),
        P(None, GRP_CTX, "wid", None),
        P(None, GRP_CTX, "wid", None),
        P(),
        P(),
        P("wid", GRP_CTX),
        P("wid", GRP_CTX),
        P("wid", GRP_CTX),
        P(GRP_CTX),
        P(GRP_CTX, "wid"),
        P("wid"),
    )
    out_specs = (P("wid", GRP_CTX), P("wid", GRP_CTX), P(GRP_CTX), P(GRP_CTX, "wid"), P("wid"))
    return jax.shard_map(body, mesh=torus, in_specs=in_specs, out_specs=out_specs, check_vma=False)
```

profile of v0, /device:TPU:32, one launch (start us, length us, event | category | flops | bytes accessed | tf_op | source)
XLA Modules:
  0.0 675.0 jit_solution(17610328824982261202)
XLA Ops:
  14.5 4.4 all-gather.1
  19.2 34.9 %all-gather.16.cloned.1.call-done = bf16[8,64,2,8,128]{4,3,2,1,0:T(8,128)(2,1)} async-done(((bf16[4,64,2,8,128]{4,3,2,1,0:T(8,128)(2,1)}), bf16[8,64,2,8,128]{4,3,2,1,0:T(8,128)(2,1)}) %all-gather.16.cloned.1.call-update) | async-done | bytes 2097168 | tf_op jit(solution)/shard_map/all_gather | solution.py:14
  54.1 3.9 fusion.1
  58.1 4.4 all-gather.2
  64.8 11.1 %all-gather.10.cloned.1.call-done = bf16[2,4,64,2,8,128]{5,4,3,2,1,0:T(8,128)(2,1)} async-done(((bf16[1,4,64,2,8,128]{5,4,3,2,1,0:T(8,128)(2,1)}), bf16[2,4,64,2,8,128]{5,4,3,2,1,0:T(8,128)(2,1)}) %all-gather.10.cloned.1.call-update) | async-done | bytes 2097168 | tf_op jit(solution)/shard_map/all_gather | solution.py:14
  75.9 4.0 add_convert_fusion.1
  81.8 15.0 %all_gather.62 = bf16[4,4,64,2,8]{2,4,3,1,0:T(8,128)(2,1)S(1)} all-gather(bf16[1,4,64,2,8]{2,4,3,1,0:T(8,128)(2,1)S(1)} %get-tuple-element.34), channel_id=1, replica_groups=mesh['grp_0'=2,'grp_1'=2,'ctx_0'=4,'ctx_1'=4,'wid'=4] {'ctx_0'}, dimensions={0}, use_global_device_ids=true | all-gather | bytes 40960 | tf_op jit(solution)/shard_map/all_gather | solution.py:14
  97.8 69.0 %all-gather.12.cloned.1.call-done = bf16[4,4,64,2,8,128]{5,4,3,2,1,0:T(8,128)(2,1)} async-done(((bf16[1,4,64,2,8,128]{5,4,3,2,1,0:T(8,128)(2,1)}), bf16[4,4,64,2,8,128]{5,4,3,2,1,0:T(8,128)(2,1)}) %all-gather.12.cloned.1.call-update) | async-done | bytes 4194320 | tf_op jit(solution)/shard_map/all_gather | solution.py:14
  166.8 7.6 %add_convert_fusion = bf16[1,4,64,2,8,128]{5,4,3,2,1,0:T(8,128)(2,1)} fusion(bf16[4,4,64,2,8,128]{5,4,3,2,1,0:T(8,128)(2,1)} %all-gather.12.cloned.1.call-done, f32[4,64,2,8]{3,2,1,0:T(2,128)S(1)} %copy.104, f32[4,64,2,8]{3,2,1,0:T(2,128)S(1)} %copy.103, f32[4,64,2,8]{3,2,1,0:T(2,128)S(1)} %copy.102, f32[4,64,2,8]{3,2,1,0:T(2,128)S(1)} %copy.101, ...), kind=kLoop, calls=%fused_computation.12 | loop fusion | flops 7340032 | bytes 5341184 | tf_op jit(solution)/shard_map/convert_element_type | solution.py:14
  174.5 13.7 %all_gather.67 = bf16[4,4,64,2,8]{2,4,3,1,0:T(8,128)(2,1)S(1)} all-gather(bf16[1,4,64,2,8]{2,4,3,1,0:T(8,128)(2,1)S(1)} %get-tuple-element.35), channel_id=1, replica_groups=mesh['grp_0'=2,'grp_1'=2,'ctx_0'=4,'ctx_1'=4,'wid'=4] {'ctx_0'}, dimensions={0}, use_global_device_ids=true | all-gather | bytes 40960 | tf_op jit(solution)/shard_map/all_gather | solution.py:14
  188.2 12.9 %all_gather.64 = bf16[4,4,64,2,8]{2,4,3,1,0:T(8,128)(2,1)S(1)} all-gather(bf16[1,4,64,2,8]{2,4,3,1,0:T(8,128)(2,1)S(1)} %get-tuple-element.28), channel_id=1, replica_groups=mesh['grp_0'=2,'grp_1'=2,'ctx_0'=4,'ctx_1'=4,'wid'=4] {'ctx_1'}, dimensions={0}, use_global_device_ids=true | all-gather | bytes 40960 | tf_op jit(solution)/shard_map/all_gather | solution.py:14
  201.0 12.2 %all_gather.68 = bf16[4,4,64,2,8]{2,4,3,1,0:T(8,128)(2,1)S(1)} all-gather(bf16[1,4,64,2,8]{2,4,3,1,0:T(8,128)(2,1)S(1)} %get-tuple-element.29), channel_id=1, replica_groups=mesh['grp_0'=2,'grp_1'=2,'ctx_0'=4,'ctx_1'=4,'wid'=4] {'ctx_1'}, dimensions={0}, use_global_device_ids=true | all-gather | bytes 40960 | tf_op jit(solution)/shard_map/all_gather | solution.py:14
  229.2 4.9 slice_convert_fusion.3
  234.2 2.7 reshape.388
  243.8 9.3 %convolution_convert_fusion.5 = bf16[256,80]{0,1:T(8,128)(2,1)S(1)} fusion(bf16[2048,80]{0,1:T(8,128)(2,1)S(1)} %copy-done.4, f32[256,2048]{1,0:T(8,128)} %div.15, f32[256,2048]{1,0:T(8,128)} %reshape.395, f32[256,2048]{1,0:T(8,128)} %mul.320, f32[256,2048]{1,0:T(8,128)} %mul.317, f32[256,2048]{1,0:T(8,128)} %reshape.393, f32[256,2048]{1,0:T(8,128)} %mul.314, ...), kind=kOutput, calls=%fused_computation.24 | convolution fusion | flops 89673728 | bytes 23437312 | tf_op jit(solution)/shard_map/dot_general | solution.py:111
  253.2 9.8 %all_to_all.39 = bf16[4,64,80]{2,1,0:T(8,128)(2,1)S(1)} all-to-all(bf16[4,64,80]{2,1,0:T(8,128)(2,1)S(1)} %bitcast.336), channel_id=1, replica_groups=mesh['grp_0'=2,'grp_1'=2,'ctx_0'=4,'ctx_1'=4,'wid'=4] {'wid'}, dimensions={0} | all-to-all | bytes 81920 | tf_op jit(solution)/shard_map/all_to_all | solution.py:35
  263.0 158.3 %all-gather.3 = bf16[64,80,64]{1,2,0:T(8,128)(2,1)S(1)} all-gather(bf16[1,80,64]{1,2,0:T(8,128)(2,1)S(1)} %bitcast.339), channel_id=1, replica_groups=mesh['grp_0'=2,'grp_1'=2,'ctx_0'=4,'ctx_1'=4,'wid'=4] {'grp_0','grp_1','..., dimensions={0}, use_global_device_ids=true | all-gather | bytes 665600 | tf_op jit(solution)/shard_map/all_gather | solution.py:114
  424.2 13.2 %all_to_all.40 = bf16[64,4,1280]{2,0,1:T(8,128)(2,1)S(1)} all-to-all(bf16[64,4,1280]{2,0,1:T(8,128)(2,1)S(1)} %bitcast.335), channel_id=1, replica_groups=mesh['grp_0'=2,'grp_1'=2,'ctx_0'=4,'ctx_1'=4,'wid'=4] {'wid'}, dimensions={1} | all-to-all | bytes 1310720 | tf_op jit(solution)/shard_map/all_to_all | solution.py:115
  438.1 12.0 %all_to_all.41 = bf16[4,256,384]{2,1,0:T(8,128)(2,1)S(1)} all-to-all(bf16[4,256,384]{2,1,0:T(8,128)(2,1)S(1)} %broadcast_in_dim.46), channel_id=1, replica_groups=mesh['grp_0'=2,'grp_1'=2,'ctx_0'=4,'ctx_1'=4,'wid'=4] {'wid'}, dimensions={0} | all-to-all | bytes 1572864 | tf_op jit(solution)/shard_map/all_to_all | solution.py:41
  452.4 6.4 all-to-all-start.3
  458.7 33.8 %all-to-all-done.3 = f32[64,4,1280]{2,1,0:T(4,128)S(1)} async-done(((f32[64,4,1280]{2,1,0:T(4,128)}), f32[64,4,1280]{2,1,0:T(4,128)S(1)}, u32[]{:S(2)}, u32[]{:S(2)}) %all-to-all-start.3) | async-done | bytes 1310752 | tf_op jit(solution)/shard_map/all_to_all | solution.py:51
  492.8 156.8 %all-gather.4 = bf16[64,4,1280]{2,1,0:T(4,128)(2,1)S(1)} all-gather(bf16[1,4,1280]{2,1,0:T(4,128)(2,1)S(1)} %fusion.78), channel_id=1, replica_groups=mesh['grp_0'=2,'grp_1'=2,'ctx_0'=4,'ctx_1'=4,'wid'=4] {'grp_0','grp_1','..., dimensions={0}, use_global_device_ids=true | all-gather | bytes 665600 | tf_op jit(solution)/shard_map/all_gather | solution.py:128
  651.3 4.2 all-to-all-start.4
  657.8 7.2 %all-to-all-done.4 = bf16[4,256,384]{2,1,0:T(8,128)(2,1)} async-done(((bf16[4,256,384]{2,1,0:T(8,128)(2,1)}), bf16[4,256,384]{2,1,0:T(8,128)(2,1)}, u32[]{:S(2)}, u32[]{:S(2)}) %all-to-all-start.4) | async-done | bytes 786464 | tf_op jit(solution)/shard_map/all_to_all | solution.py:41
  (105 shorter events, 49.0 us)
Async XLA Ops:
  7.2 2.0 copy-start
  7.2 46.9 %all-gather.16.cloned.1.call-start = ((), (), s32[]{:S(2)}) async-start(), calls=%async_computation.8 | async-start | bytes 3145728 | tf_op jit(solution)/shard_map/all_gather | solution.py:14
  11.3 1.5 copy-start.5
  14.4 61.5 %all-gather.10.cloned.1.call-start = ((), (), s32[]{:S(2)}) async-start(), calls=%async_computation.5 | async-start | bytes 3145728 | tf_op jit(solution)/shard_map/all_gather | solution.py:14
  58.1 108.7 %all-gather.12.cloned.1.call-start = ((), (), s32[]{:S(2)}) async-start(), calls=%async_computation.6 | async-start | bytes 5242880 | tf_op jit(solution)/shard_map/all_gather | solution.py:14
  79.9 149.4 %all-gather.14.cloned.1.call-start = ((), (), s32[]{:S(2)}) async-start(), calls=%async_computation.7 | async-start | bytes 5242880 | tf_op jit(solution)/shard_map/all_gather | solution.py:14
  242.3 1.5 copy-start.4
  243.8 19.2 %copy-start.7 = (bf16[64,80]{1,0:T(8,128)(2,1)S(1)}, bf16[64,80]{1,0:T(8,128)(2,1)}, u32[]{:S(2)}) copy-start(bf16[64,80]{1,0:T(8,128)(2,1)} %param.16) | copy-start | bytes 30724
  263.0 161.1 %copy-start.6 = (bf16[64,80]{1,0:T(8,128)(2,1)}, bf16[64,80]{1,0:T(8,128)(2,1)S(1)}, u32[]{:S(2)}) copy-start(bf16[64,80]{1,0:T(8,128)(2,1)S(1)} %add_convert_fusion.2) | copy-start | bytes 30724
  422.0 15.4 %copy-start.3 = (bf16[1280,384]{1,0:T(8,128)(2,1)S(1)}, bf16[1280,384]{1,0:T(8,128)(2,1)}, u32[]{:S(2)}) copy-start(bf16[1280,384]{1,0:T(8,128)(2,1)} %param.18) | copy-start | bytes 2949124
  438.0 12.2 %copy-start.2 = (bf16[384,1280]{1,0:T(8,128)(2,1)S(1)}, bf16[384,1280]{1,0:T(8,128)(2,1)}, u32[]{:S(2)}) copy-start(bf16[384,1280]{1,0:T(8,128)(2,1)} %param.20) | copy-start | bytes 2949124
  438.0 12.2 %copy-start.8 = (f32[384]{0:T(512)S(1)}, f32[384]{0:T(512)}, u32[]{:S(2)}) copy-start(f32[384]{0:T(512)} %param.19) | copy-start | bytes 4612
  452.4 40.4 %copy-start.9 = (f32[1280]{0:T(1024)S(1)}, f32[1280]{0:T(1024)}, u32[]{:S(2)}) copy-start(f32[1280]{0:T(1024)} %param.21) | copy-start | bytes 15364
  452.4 40.2 %all-to-all-start.3 = ((f32[64,4,1280]{2,1,0:T(4,128)}), f32[64,4,1280]{2,1,0:T(4,128)S(1)}, u32[]{:S(2)}, u32[]{:S(2)}) async-start(f32[64,4,1280]{2,1,0:T(4,128)} %reshape.379), calls=%async_computation.3 | async-start | bytes 2621440 | tf_op jit(solution)/shard_map/all_to_all | solution.py:51
  651.3 13.7 %all-to-all-start.4 = ((bf16[4,256,384]{2,1,0:T(8,128)(2,1)}), bf16[4,256,384]{2,1,0:T(8,128)(2,1)}, u32[]{:S(2)}, u32[]{:S(2)}) async-start(bf16[4,256,384]{2,1,0:T(8,128)(2,1)} %broadcast_in_dim.78), calls=%async_computation.4 | async-start | bytes 1572864 | tf_op jit(solution)/shard_map/all_to_all | solution.py:41
  656.2 12.3 %copy-start.1 = (bf16[256,16,128]{2,1,0:T(8,128)(2,1)S(1)}, bf16[256,16,128]{2,1,0:T(8,128)(2,1)}, u32[]{:S(2)}) copy-start(bf16[256,16,128]{2,1,0:T(8,128)(2,1)} %param.11) | copy-start | bytes 3145732
Sparse Core Ops, SparseCore 0:
  14.5 39.5 all-gather.15
  58.2 17.6 all-gather.9
  80.0 86.7 all-gather.11
  174.6 51.0 all-gather.13
where the time goes:
time: 676 us; the launch traced here: 675 us
  blocking collectives  416 us (62%)
  waiting for transfers between devices  156 us (23%)
  local copies, waits for them, and re-layouts  35.3 us (5%)
  other arithmetic  25.7 us (4%)
  matrix products  16.5 us (2%)
  between operations  14.2 us (2%)
  starting transfers between devices  10.7 us (2%)
    all_gather x1, blocking collectives, body(): wide_rows = lax.all_gather(layer_out, GRP_CTX, axis=1, tiled=True)  158 us
    all_gather x1, blocking collectives, body(): error_all = lax.all_gather(scaled_error, GRP_CTX, axis=0, tiled=True)  157 us
    all_gather x4, waiting for transfers between devices, combined_by_axis(): lax.all_gather(part.astype(kind), axis)  115 us
    all_gather x8, blocking collectives, combined_by_axis(): lax.all_gather(part.astype(kind), axis)  66.3 us
    all_to_all x1, waiting for transfers between devices, sent_and_summed(): lax.all_to_all(in_blocks(shard, dim, length), axis, 0, 0, tiled=True)  33.8 us
    convert_element_type x7, other arithmetic, combined_by_axis(): part.astype(kind)  15.6 us
  transfers between devices with their start and end apart: 6, of which 5 were waited for; matrix products, arithmetic and copies ran while one was open for 3% of the time, Pallas kernels for 0%

commit v1 on v0

--- a/solution.py
+++ b/solution.py
@@ -1,3 +1,4 @@
+import functools
 import jax
 import jax.numpy as jnp
 from jax import lax
@@ -6,6 +7,15 @@
 
 HD = 128
 GRP_CTX = ("grp_0", "grp_1", "ctx_0", "ctx_1")
+
+
+def register_the_halves(content, dev_axis, which_dim):
+    e_next = jnp.stack([content for _ in range(lax.axis_size(dev_axis))])
+    tile_out = jnp.concatenate(lax.all_to_all(e_next, dev_axis, 0, 0), axis=which_dim)
+    return tile_out
+
+
+series_all_shape = functools.partial(register_the_halves, dev_axis=GRP_CTX, which_dim=1)
 
 
 def combined_by_axis(shard, axes, combine):
@@ -111,7 +121,7 @@
     projected = jnp.dot(attention, out_weight, preferred_element_type=jnp.float32)
     mixed = summed_on_arrival(projected.astype(jnp.bfloat16), "wid", 0)
     layer_out = (mixed + resid.astype(jnp.float32)).astype(jnp.bfloat16)
-    wide_rows = lax.all_gather(layer_out, GRP_CTX, axis=1, tiled=True)
+    wide_rows = series_all_shape(layer_out)
     block = lax.all_to_all(wide_rows, "wid", split_axis=1, concat_axis=0, tiled=True)
     enc_part = jnp.dot(block, enc_weight, preferred_element_type=jnp.float32)
     preact = taken_together(enc_part.astype(jnp.bfloat16), "wid").astype(jnp.float32) + enc_bias

time: 676 us -> 556 us (0.82)
  blocking collectives: 416 us -> 297 us
    all_gather x1 -> x0, blocking collectives: 158 us -> none  [body(): wide_rows = lax.all_gather(layer_out, GRP_CTX, axis=1, tiled=True)]
    all_to_all x0 -> x1, blocking collectives: none -> 35.4 us  [register_the_halves(): lax.all_to_all(e_next, dev_axis, 0, 0)]
  transfers between devices with their start and end apart: 6 -> 6, of which waited for: 5 -> 5; matrix products, arithmetic and copies ran while one was open for 3% -> 4% of each run, Pallas kernels for 0% -> 0%
where the time goes in v1:
time: 556 us; the launch traced here: 555 us
  blocking collectives  297 us (53%)
  waiting for transfers between devices  156 us (28%)
  local copies, waits for them, and re-layouts  34.8 us (6%)
  other arithmetic  25.7 us (5%)
  matrix products  16.5 us (3%)
  between operations  14.2 us (3%)
  starting transfers between devices  10.4 us (2%)
    all_gather x1, blocking collectives, body(): error_all = lax.all_gather(scaled_error, GRP_CTX, axis=0, tiled=True)  157 us
    all_gather x4, waiting for transfers between devices, combined_by_axis(): lax.all_gather(part.astype(kind), axis)  115 us
    all_gather x8, blocking collectives, combined_by_axis(): lax.all_gather(part.astype(kind), axis)  66.3 us
    all_to_all x1, blocking collectives, register_the_halves(): lax.all_to_all(e_next, dev_axis, 0, 0)  35.4 us
    all_to_all x1, waiting for transfers between devices, sent_and_summed(): lax.all_to_all(in_blocks(shard, dim, length), axis, 0, 0, tiled=True)  33.8 us
    convert_element_type x7, other arithmetic, combined_by_axis(): part.astype(kind)  15.6 us
    all_to_all x1, blocking collectives, from_everyone(): return lax.all_to_all(copies, axis, split_axis=0, concat_axis=0, tiled=True)  14.7 us
    all_to_all x1, blocking collectives, body(): lax.all_to_all(wide_rows, 'wid', split_axis=1, concat_axis=0, tiled=True)  13.9 us
  transfers between devices with their start and end apart: 6, of which 5 were waited for; matrix products, arithmetic and copies ran while one was open for 4% of the time, Pallas kernels for 0%

profile of v1, /device:TPU:32, one launch (start us, length us, event | category | flops | bytes accessed | tf_op | source)
XLA Modules:
  0.0 554.7 jit_solution(16289684685825562323)
XLA Ops:
  14.5 4.4 all-gather.1
  19.2 34.9 %all-gather.15.cloned.1.call-done = bf16[8,64,2,8,128]{4,3,2,1,0:T(8,128)(2,1)} async-done(((bf16[4,64,2,8,128]{4,3,2,1,0:T(8,128)(2,1)}), bf16[8,64,2,8,128]{4,3,2,1,0:T(8,128)(2,1)}) %all-gather.15.cloned.1.call-update) | async-done | bytes 2097168 | tf_op jit(solution)/shard_map/all_gather | solution.py:24
  54.1 3.9 fusion.1
  58.1 4.4 all-gather.2
  64.8 11.1 %all-gather.9.cloned.1.call-done = bf16[2,4,64,2,8,128]{5,4,3,2,1,0:T(8,128)(2,1)} async-done(((bf16[1,4,64,2,8,128]{5,4,3,2,1,0:T(8,128)(2,1)}), bf16[2,4,64,2,8,128]{5,4,3,2,1,0:T(8,128)(2,1)}) %all-gather.9.cloned.1.call-update) | async-done | bytes 2097168 | tf_op jit(solution)/shard_map/all_gather | solution.py:24
  75.9 4.0 add_convert_fusion.1
  81.8 15.0 %all_gather.59 = bf16[4,4,64,2,8]{2,4,3,1,0:T(8,128)(2,1)S(1)} all-gather(bf16[1,4,64,2,8]{2,4,3,1,0:T(8,128)(2,1)S(1)} %get-tuple-element.34), channel_id=1, replica_groups=mesh['grp_0'=2,'grp_1'=2,'ctx_0'=4,'ctx_1'=4,'wid'=4] {'ctx_0'}, dimensions={0}, use_global_device_ids=true | all-gather | bytes 40960 | tf_op jit(solution)/shard_map/all_gather | solution.py:24
  97.8 69.0 %all-gather.11.cloned.1.call-done = bf16[4,4,64,2,8,128]{5,4,3,2,1,0:T(8,128)(2,1)} async-done(((bf16[1,4,64,2,8,128]{5,4,3,2,1,0:T(8,128)(2,1)}), bf16[4,4,64,2,8,128]{5,4,3,2,1,0:T(8,128)(2,1)}) %all-gather.11.cloned.1.call-update) | async-done | bytes 4194320 | tf_op jit(solution)/shard_map/all_gather | solution.py:24
  166.8 7.6 %add_convert_fusion = bf16[1,4,64,2,8,128]{5,4,3,2,1,0:T(8,128)(2,1)} fusion(bf16[4,4,64,2,8,128]{5,4,3,2,1,0:T(8,128)(2,1)} %all-gather.11.cloned.1.call-done, f32[4,64,2,8]{3,2,1,0:T(2,128)S(1)} %copy.103, f32[4,64,2,8]{3,2,1,0:T(2,128)S(1)} %copy.102, f32[4,64,2,8]{3,2,1,0:T(2,128)S(1)} %copy.101, f32[4,64,2,8]{3,2,1,0:T(2,128)S(1)} %copy.100, ...), kind=kLoop, calls=%fused_computation.12 | loop fusion | flops 7340032 | bytes 5341184 | tf_op jit(solution)/shard_map/convert_element_type | solution.py:24
  174.5 13.7 %all_gather.64 = bf16[4,4,64,2,8]{2,4,3,1,0:T(8,128)(2,1)S(1)} all-gather(bf16[1,4,64,2,8]{2,4,3,1,0:T(8,128)(2,1)S(1)} %get-tuple-element.35), channel_id=1, replica_groups=mesh['grp_0'=2,'grp_1'=2,'ctx_0'=4,'ctx_1'=4,'wid'=4] {'ctx_0'}, dimensions={0}, use_global_device_ids=true | all-gather | bytes 40960 | tf_op jit(solution)/shard_map/all_gather | solution.py:24
  188.2 12.9 %all_gather.61 = bf16[4,4,64,2,8]{2,4,3,1,0:T(8,128)(2,1)S(1)} all-gather(bf16[1,4,64,2,8]{2,4,3,1,0:T(8,128)(2,1)S(1)} %get-tuple-element.28), channel_id=1, replica_groups=mesh['grp_0'=2,'grp_1'=2,'ctx_0'=4,'ctx_1'=4,'wid'=4] {'ctx_1'}, dimensions={0}, use_global_device_ids=true | all-gather | bytes 40960 | tf_op jit(solution)/shard_map/all_gather | solution.py:24
  201.0 12.2 %all_gather.65 = bf16[4,4,64,2,8]{2,4,3,1,0:T(8,128)(2,1)S(1)} all-gather(bf16[1,4,64,2,8]{2,4,3,1,0:T(8,128)(2,1)S(1)} %get-tuple-element.29), channel_id=1, replica_groups=mesh['grp_0'=2,'grp_1'=2,'ctx_0'=4,'ctx_1'=4,'wid'=4] {'ctx_1'}, dimensions={0}, use_global_device_ids=true | all-gather | bytes 40960 | tf_op jit(solution)/shard_map/all_gather | solution.py:24
  229.2 4.9 slice_convert_fusion.3
  234.2 2.7 reshape.396
  243.8 9.3 %convolution_convert_fusion.5 = bf16[256,80]{0,1:T(8,128)(2,1)S(1)} fusion(bf16[2048,80]{0,1:T(8,128)(2,1)S(1)} %copy-done.4, f32[256,2048]{1,0:T(8,128)} %div.15, f32[256,2048]{1,0:T(8,128)} %reshape.403, f32[256,2048]{1,0:T(8,128)} %mul.320, f32[256,2048]{1,0:T(8,128)} %mul.317, f32[256,2048]{1,0:T(8,128)} %reshape.401, f32[256,2048]{1,0:T(8,128)} %mul.314, ...), kind=kOutput, calls=%fused_computation.24 | convolution fusion | flops 89673728 | bytes 23437312 | tf_op jit(solution)/shard_map/dot_general | solution.py:121
  253.2 9.8 %all_to_all.44 = bf16[4,64,80]{2,1,0:T(8,128)(2,1)S(1)} all-to-all(bf16[4,64,80]{2,1,0:T(8,128)(2,1)S(1)} %bitcast.326), channel_id=1, replica_groups=mesh['grp_0'=2,'grp_1'=2,'ctx_0'=4,'ctx_1'=4,'wid'=4] {'wid'}, dimensions={0} | all-to-all | bytes 81920 | tf_op jit(solution)/shard_map/all_to_all | solution.py:45
  263.3 35.4 %all_to_all.45 = bf16[64,64,80]{2,1,0:T(8,128)(2,1)S(1)} all-to-all(bf16[64,64,80]{2,1,0:T(8,128)(2,1)S(1)} %stack.2), channel_id=1, replica_groups=mesh['grp_0'=2,'grp_1'=2,'ctx_0'=4,'ctx_1'=4,'wid'=4] {'grp_0','grp_1','..., dimensions={0} | all-to-all | bytes 1310720 | tf_op jit(solution)/shard_map/all_to_all | solution.py:14
  300.8 13.9 %all_to_all.46 = bf16[64,4,1280]{2,0,1:T(8,128)(2,1)S(1)} all-to-all(bf16[64,4,1280]{2,0,1:T(8,128)(2,1)S(1)} %copy.113), channel_id=1, replica_groups=mesh['grp_0'=2,'grp_1'=2,'ctx_0'=4,'ctx_1'=4,'wid'=4] {'wid'}, dimensions={1} | all-to-all | bytes 1310720 | tf_op jit(solution)/shard_map/all_to_all | solution.py:125
  315.4 14.7 %all_to_all.47 = bf16[4,256,384]{2,1,0:T(8,128)(2,1)S(1)} all-to-all(bf16[4,256,384]{2,1,0:T(8,128)(2,1)S(1)} %broadcast_in_dim.46), channel_id=1, replica_groups=mesh['grp_0'=2,'grp_1'=2,'ctx_0'=4,'ctx_1'=4,'wid'=4] {'wid'}, dimensions={0} | all-to-all | bytes 1572864 | tf_op jit(solution)/shard_map/all_to_all | solution.py:51
  332.3 6.1 %all-to-all-start.4 = ((f32[64,4,1280]{2,1,0:T(4,128)}), f32[64,4,1280]{2,1,0:T(4,128)S(1)}, u32[]{:S(2)}, u32[]{:S(2)}) async-start(f32[64,4,1280]{2,1,0:T(4,128)} %reshape.387), calls=%async_computation.4 | async-start | bytes 2621440 | tf_op jit(solution)/shard_map/all_to_all | solution.py:61
  338.4 33.8 %all-to-all-done.4 = f32[64,4,1280]{2,1,0:T(4,128)S(1)} async-done(((f32[64,4,1280]{2,1,0:T(4,128)}), f32[64,4,1280]{2,1,0:T(4,128)S(1)}, u32[]{:S(2)}, u32[]{:S(2)}) %all-to-all-start.4) | async-done | bytes 1310752 | tf_op jit(solution)/shard_map/all_to_all | solution.py:61
  372.5 156.8 %all-gather.3 = bf16[64,4,1280]{2,1,0:T(4,128)(2,1)S(1)} all-gather(bf16[1,4,1280]{2,1,0:T(4,128)(2,1)S(1)} %fusion.78), channel_id=1, replica_groups=mesh['grp_0'=2,'grp_1'=2,'ctx_0'=4,'ctx_1'=4,'wid'=4] {'grp_0','grp_1','..., dimensions={0}, use_global_device_ids=true | all-gather | bytes 665600 | tf_op jit(solution)/shard_map/all_gather | solution.py:138
  530.9 4.2 all-to-all-start.5
  537.4 7.2 %all-to-all-done.5 = bf16[4,256,384]{2,1,0:T(8,128)(2,1)} async-done(((bf16[4,256,384]{2,1,0:T(8,128)(2,1)}), bf16[4,256,384]{2,1,0:T(8,128)(2,1)}, u32[]{:S(2)}, u32[]{:S(2)}) %all-to-all-start.5) | async-done | bytes 786464 | tf_op jit(solution)/shard_map/all_to_all | solution.py:51
  (106 shorter events, 48.5 us)
Async XLA Ops:
  7.2 2.0 copy-start
  7.2 46.9 %all-gather.15.cloned.1.call-start = ((), (), s32[]{:S(2)}) async-start(), calls=%async_computation.9 | async-start | bytes 3145728 | tf_op jit(solution)/shard_map/all_gather | solution.py:24
  11.3 1.5 copy-start.5
  14.4 61.5 %all-gather.9.cloned.1.call-start = ((), (), s32[]{:S(2)}) async-start(), calls=%async_computation.6 | async-start | bytes 3145728 | tf_op jit(solution)/shard_map/all_gather | solution.py:24
  58.1 108.7 %all-gather.11.cloned.1.call-start = ((), (), s32[]{:S(2)}) async-start(), calls=%async_computation.7 | async-start | bytes 5242880 | tf_op jit(solution)/shard_map/all_gather | solution.py:24
  79.9 149.4 %all-gather.13.cloned.1.call-start = ((), (), s32[]{:S(2)}) async-start(), calls=%async_computation.8 | async-start | bytes 5242880 | tf_op jit(solution)/shard_map/all_gather | solution.py:24
  242.3 1.5 copy-start.4
  243.8 19.2 %copy-start.7 = (bf16[64,80]{1,0:T(8,128)(2,1)S(1)}, bf16[64,80]{1,0:T(8,128)(2,1)}, u32[]{:S(2)}) copy-start(bf16[64,80]{1,0:T(8,128)(2,1)} %param.16) | copy-start | bytes 30724
  263.0 36.4 %copy-start.6 = (bf16[64,80]{1,0:T(8,128)(2,1)}, bf16[64,80]{1,0:T(8,128)(2,1)S(1)}, u32[]{:S(2)}) copy-start(bf16[64,80]{1,0:T(8,128)(2,1)S(1)} %add_convert_fusion.2) | copy-start | bytes 30724
  299.4 15.3 %copy-start.3 = (bf16[1280,384]{1,0:T(8,128)(2,1)S(1)}, bf16[1280,384]{1,0:T(8,128)(2,1)}, u32[]{:S(2)}) copy-start(bf16[1280,384]{1,0:T(8,128)(2,1)} %param.18) | copy-start | bytes 2949124
  315.3 14.9 %copy-start.2 = (bf16[384,1280]{1,0:T(8,128)(2,1)S(1)}, bf16[384,1280]{1,0:T(8,128)(2,1)}, u32[]{:S(2)}) copy-start(bf16[384,1280]{1,0:T(8,128)(2,1)} %param.20) | copy-start | bytes 2949124
  315.3 14.9 %copy-start.8 = (f32[384]{0:T(512)S(1)}, f32[384]{0:T(512)}, u32[]{:S(2)}) copy-start(f32[384]{0:T(512)} %param.19) | copy-start | bytes 4612
  332.3 40.2 %copy-start.9 = (f32[1280]{0:T(1024)S(1)}, f32[1280]{0:T(1024)}, u32[]{:S(2)}) copy-start(f32[1280]{0:T(1024)} %param.21) | copy-start | bytes 15364
  332.3 39.9 %all-to-all-start.4 = ((f32[64,4,1280]{2,1,0:T(4,128)}), f32[64,4,1280]{2,1,0:T(4,128)S(1)}, u32[]{:S(2)}, u32[]{:S(2)}) async-start(f32[64,4,1280]{2,1,0:T(4,128)} %reshape.387), calls=%async_computation.4 | async-start | bytes 2621440 | tf_op jit(solution)/shard_map/all_to_all | solution.py:61
  530.9 13.7 %all-to-all-start.5 = ((bf16[4,256,384]{2,1,0:T(8,128)(2,1)}), bf16[4,256,384]{2,1,0:T(8,128)(2,1)}, u32[]{:S(2)}, u32[]{:S(2)}) async-start(bf16[4,256,384]{2,1,0:T(8,128)(2,1)} %broadcast_in_dim.78), calls=%async_computation.5 | async-start | bytes 1572864 | tf_op jit(solution)/shard_map/all_to_all | solution.py:51
  535.8 12.3 %copy-start.1 = (bf16[256,16,128]{2,1,0:T(8,128)(2,1)S(1)}, bf16[256,16,128]{2,1,0:T(8,128)(2,1)}, u32[]{:S(2)}) copy-start(bf16[256,16,128]{2,1,0:T(8,128)(2,1)} %param.11) | copy-start | bytes 3145732
Sparse Core Ops, SparseCore 0:
  14.5 39.5 all-gather.14
  58.2 17.6 all-gather.8
  80.0 86.7 all-gather.10
  174.6 51.0 all-gather.12
